TPU v7x, 256 devices: a whole 4x4x8 slice. The times are simulated.
256 devices in a mesh: gx: 64 (over z, y, core), gy: 4 (over x).
Axes of the slice: x: 4, y: 4, z: 8, core: 2. Of those that a mesh axis runs over, the one named last changes fastest.
Arguments:
- velocity_u: float32 [4096, 16, 2048], P('gx', None, 'gy'), may hold values from -6 to 6
- wall_strain: float32 [4096, 16, 2048], P('gx', None, 'gy'), may hold values from -6 to 6
- damping: float32 [16, 2048], P(None, 'gy'), may hold values from 0.88 to 1
Outputs:
- second_deriv: float32 [4096, 16, 2048], P('gx', None, 'gy')
- cosine_coeffs: float32 [4096, 16, 2048], P('gx', None, 'gy')
- pressure: float32 [4096, 16, 2048], P('gx', None, 'gy')
All inputs are finite; a program needn't handle non-finite values.
Results may differ from a plain program's by a relative error of at most 0.0003.
Values sent between devices are 32-bit elements; how exact they have to be, the bound alone decides.
A program may use at most 128 MiB of HBM per device.

v0:
```python
import math

import jax
import jax.numpy as jnp
from jax import lax
from jax.sharding import Mesh
from jax.sharding import PartitionSpec as P

NY = 2048
GX = ("gx_0", "gx_1", "gx_2")


highest = lax.Precision.HIGHEST


def padded_2(shard, sides, width):
    for axis, dim in sides:
        count, length = (lax.axis_size(axis), shard.shape[dim])
        up = [(i, (i + 1) % count) for i in range(count - 1)]
        down = [(j, i) for i, j in up]
        last = lax.slice_in_dim(shard, length - width, length, axis=dim)
        first = lax.slice_in_dim(shard, 0, width, axis=dim)
        before = lax.ppermute(last, axis, up)
        after = lax.ppermute(first, axis, down)
        shard = jnp.concatenate([before, shard, after], axis=dim)
    return shard


def cut_along(shard, dim, count):
    dims = shard.shape
    parts = shard.reshape(*dims[:dim], count, dims[dim] // count, *dims[dim + 1 :])
    return jnp.moveaxis(parts, dim, 0)


def sum_at_owner(shard, axis, dim):
    parts = cut_along(shard, dim, lax.axis_size(axis))
    arrived = lax.all_to_all(parts, axis, split_axis=0, concat_axis=0, tiled=True)
    return arrived.sum(axis=0)


def nothing_yet(shard, identity):
    return jax.tree.map(
        lambda part, zero: jnp.zeros_like(part) + jnp.asarray(zero, part.dtype), shard, identity
    )


def carried_in(shard, axes, combine, identity):
    before = start = nothing_yet(shard, identity)
    so_far = shard
    for axis in reversed(axes):
        count, index = (lax.axis_size(axis), lax.axis_index(axis))
        pieces = jax.tree.map(lambda part: lax.all_gather(part, axis), so_far)
        inside, so_far = (start, start)
        for k in range(count):
            passed = k < index
            so_far = combine(so_far, jax.tree.map(lambda part: part[k], pieces))
            inside = jax.tree.map(lambda new, old: jnp.where(passed, new, old), so_far, inside)
        before = combine(inside, before)
    return before


def all_in_one(shard, axis):
    leaves = jax.tree.leaves(shard)
    sequence = sorted(range(len(leaves)), key=lambda k: -leaves[k].size)
    width = (1, *leaves[sequence[0]].shape)[-1]
    lines = [
        jnp.pad(leaves[k].reshape(-1), (0, -leaves[k].size % width)).reshape(-1, width)
        for k in sequence
    ]
    both, at, found = (lax.all_gather(jnp.concatenate(lines), axis), 0, {})
    for k, line in zip(sequence, lines):
        share = both[:, at : at + len(line)].reshape(len(both), -1)
        found[k] = share[:, : leaves[k].size].reshape(-1, *leaves[k].shape)
        at += len(line)
    numbers = iter(range(len(leaves)))
    return jax.tree.map(lambda _: found[next(numbers)], shard)


def collected_alike(shard, axis):
    leaves, found = (jax.tree.leaves(shard), {})
    for first, a in enumerate(leaves):
        if first not in found:
            alike = [k for k, b in enumerate(leaves) if b.dtype == a.dtype]
            got = (
                all_in_one([leaves[k] for k in alike], axis)
                if len(alike) > 1
                else [lax.all_gather(a, axis)]
            )
            for k, b in zip(alike, got):
                found[k] = b
    numbers = iter(range(len(leaves)))
    return jax.tree.map(lambda _: found[next(numbers)], shard)


def carried_in_2(shard, axes, combine, identity):
    before = start = nothing_yet(shard, identity)
    so_far = shard
    for axis in reversed(axes):
        count, index = (lax.axis_size(axis), lax.axis_index(axis))
        pieces = collected_alike(so_far, axis)
        inside, so_far = (start, start)
        for k in reversed(range(count)):
            passed = k > index
            so_far = combine(so_far, jax.tree.map(lambda part: part[k], pieces))
            inside = jax.tree.map(lambda new, old: jnp.where(passed, new, old), so_far, inside)
        before = combine(inside, before)
    return before


def stencil_terms(padded, cells):

    def shifted(offset):
        return padded[3 + offset : 3 + offset + cells]

    first = (
        0.75 * (shifted(1) - shifted(-1))
        - 3.0 / 20.0 * (shifted(2) - shifted(-2))
        + 1.0 / 60.0 * (shifted(3) - shifted(-3))
    )
    second = (
        1.5 * (shifted(1) + shifted(-1))
        - 3.0 / 20.0 * (shifted(2) + shifted(-2))
        + 1.0 / 90.0 * (shifted(3) + shifted(-3))
        - 49.0 / 18.0 * shifted(0)
    )
    return (first, second)


def recurse(values, factor, reverse):
    length = values.shape[0]
    stride = 1
    power = factor
    while stride < length:
        if reverse:
            carried = jnp.pad(values[stride:], ((0, stride), (0, 0)))
        else:
            carried = jnp.pad(values[:-stride], ((stride, 0), (0, 0)))
        values = values + power[None, :] * carried
        power = power * power
        stride = stride * 2
    return values


def compose(earlier, later):
    return (later[0] * earlier[0], later[0] * earlier[1] + later[1])


def cosine_table(samples, modes, length):
    phase = (samples[:, None] * 2 + 1) * modes[None, :] % (4 * length)
    return math.sqrt(2.0 / length) * jnp.cos(math.pi * phase.astype(jnp.float32) / (2.0 * length))


def body(velocity_u, wall_strain, damping):
    cells, planes, columns = velocity_u.shape
    lines = planes * columns
    padded = padded_2(velocity_u, ((GX, 0),), 3)
    first, second = stencil_terms(padded, cells)
    source = (first + wall_strain).reshape(cells * planes, columns)
    my_offset = lax.axis_index("gy") * columns
    modes = jnp.arange(columns * lax.axis_size("gy"), dtype=jnp.int32)
    samples = my_offset + jnp.arange(columns, dtype=jnp.int32)
    table = cosine_table(samples, modes, NY)
    owned = sum_at_owner(
        lax.dot_general(
            table,
            source,
            (((0,), (1,)), ((), ())),
            precision=highest,
            preferred_element_type=jnp.float32,
        ),
        "gy",
        0,
    )
    coefficients = owned.T.reshape(cells, planes, columns)
    weight = ((1.0 - damping) * (1.0 + damping)) ** 1.5
    forcing = (weight[None, :, :] * coefficients).reshape(cells, lines)
    decay_line = damping.reshape(lines)
    exponents = jnp.arange(1, cells + 1, dtype=jnp.float32)
    powers = jnp.exp(exponents[:, None] * jnp.log(decay_line)[None, :])
    block_scale = powers[-1]
    identity = (jnp.ones((lines,), jnp.float32), jnp.zeros((lines,), jnp.float32))
    local_forward = recurse(forcing, decay_line, False)
    before = carried_in((block_scale, local_forward[-1]), GX, compose, identity)
    forward_full = local_forward + powers * before[1][None, :]
    local_back = recurse(forward_full, decay_line, True)
    after = carried_in_2((block_scale, local_back[0]), GX, compose, identity)
    pressure = local_back + powers[::-1] * after[1][None, :]
    return (second, coefficients, pressure.reshape(cells, planes, columns))


def solution(mesh):
    finer = Mesh(mesh.devices.reshape(8, 4, 2, mesh.shape["gy"]), ("gx_0", "gx_1", "gx_2", "gy"))
    placed = (P(GX, None, "gy"), P(GX, None, "gy"), P(None, "gy"))
    return jax.shard_map(
        body,
        mesh=finer,
        in_specs=placed,
        out_specs=(P(GX, None, "gy"), P(GX, None, "gy"), P(GX, None, "gy")),
        check_vma=False,
    )
```

profile of v0, /device:TPU:8, one launch (start us, length us, event | category | flops | bytes accessed | tf_op | source)
XLA Modules:
  0.0 286.4 jit_solution(11999371020454057817)
XLA Ops:
  0.6 1.0 fusion.65
  1.6 1.9 collective-permute-start.1
  3.5 3.6 %collective-permute-start = (f32[3,16,512]{2,1,0:T(8,128)S(1)}, f32[3,16,512]{2,1,0:T(8,128)S(1)}, u32[]{:S(2)}, u32[]{:S(2)}) collective-permute-start(f32[3,16,512]{2,1,0:T(8,128)S(1)} %get-tuple-element.16), channel_id=1, source_target_pairs={{4,0},{8,4},{12,8},{16,12},{20,16},{24,20},{28,24},{32,28},{36,32}... | collective-permute-start | bytes 294920 | tf_op jit(solution)/shard_map/ppermute | solution.py:24
  7.2 0.3 collective-permute-done.1
  7.6 2.3 constant_dynamic-update-slice_fusion.1
  9.9 0.5 copy-done.4
  10.4 3.3 %add_add_fusion = (f32[64,16,512]{2,1,0:T(8,128)S(1)}, f32[64,16,512]{2,1,0:T(8,128)}) fusion(f32[64,16,512]{2,1,0:T(8,128)S(1)} %copy-done.4, f32[67,16,512]{2,1,0:T(8,128)S(1)} %get-tuple-element.19, f32[67,16,512]{2,1,0:T(8,128)S(1)} %constant_dynamic-update-slice_fusion, f32[64,16,512]{2,1,0:T(8,128)S(1)} %copy-done.1), kind=kLoop, calls=%fused_computation.29 | loop fusion | flops 9961472 | bytes 20971520 | tf_op jit(solution)/shard_map/add | solution.py:158
  13.7 31.3 %fusion.4 = f32[4,512,1024]{2,1,0:T(8,128)} fusion(f32[1024,512,1]{1,0,2:T(8,128)S(1)} %bitcast.316, s32[4,512]{1,0:T(4,128)S(1)} %multiply_add_fusion.14, s32[512]{0:T(512)S(1)} %multiply_add_fusion.15), kind=kOutput, calls=%fused_computation.9 | convolution fusion | flops 12900630528 | bytes 10496000 | tf_op jit(solution)/shard_map/dot_general | solution.py:164
  45.0 5.8 %all-to-all-start = ((f32[4,512,1024]{2,1,0:T(8,128)}), f32[4,512,1024]{2,1,0:T(8,128)}, u32[]{:S(2)}, u32[]{:S(2)}) async-start(f32[4,512,1024]{2,1,0:T(8,128)} %fusion.4), calls=%async_computation | async-start | bytes 16777216 | tf_op jit(solution)/shard_map/all_to_all | solution.py:37
  50.9 0.4 multiply_exponential_fusion
  51.4 20.0 %rev.3 = f32[64,8192]{1,0:T(8,128)} reverse(f32[64,8192]{1,0:T(8,128)S(1)} %multiply_exponential_fusion), dimensions={0} | reverse | bytes 4194304 | tf_op jit(solution)/shard_map/rev | solution.py:187
  71.4 2.5 all-gather.3
  73.9 71.9 %all-to-all-done = f32[4,512,1024]{2,1,0:T(8,128)} async-done(((f32[4,512,1024]{2,1,0:T(8,128)}), f32[4,512,1024]{2,1,0:T(8,128)}, u32[]{:S(2)}, u32[]{:S(2)}) %all-to-all-start) | async-done | bytes 8388640 | tf_op jit(solution)/shard_map/all_to_all | solution.py:37
  145.8 5.9 %reduce_sum.9 = f32[512,1024]{1,0:T(8,128)} reduce(f32[4,512,1024]{2,1,0:T(8,128)} %all-to-all-done, f32[]{:T(128)} %constant.25.clone.1), dimensions={0}, to_apply=%region_0.1 | reduce | flops 1572864 | bytes 10485764 | tf_op jit(solution)/shard_map/reduce_sum | solution.py:38
  151.7 1.9 copy.9
  153.6 1.7 reshape.507
  156.2 1.2 copy.13
  157.4 0.4 copy-done.3
  157.8 0.4 multiply_add_fusion.13
  159.8 1.9 all-gather.6
  161.7 11.9 %all-gather.4 = f32[4,1,8192]{2,1,0:T(1,128)S(1)} all-gather(f32[1,1,8192]{2,1,0:T(1,128)S(1)} %get-tuple-element.38), channel_id=1, replica_groups=mesh['gx_0'=8,'gx_1'=4,'gx_2'=2,'gy'=4] {'gx_1'}, dimensions={0}, use_global_device_ids=true | all-gather | bytes 163840 | tf_op jit(solution)/shard_map/all_gather | solution.py:52
  173.6 12.0 %all-gather.7 = f32[4,1,8192]{2,1,0:T(1,128)S(1)} all-gather(f32[1,1,8192]{2,1,0:T(1,128)S(1)} %bitcast.324), channel_id=1, replica_groups=mesh['gx_0'=8,'gx_1'=4,'gx_2'=2,'gy'=4] {'gx_1'}, dimensions={0}, use_global_device_ids=true | all-gather | bytes 163840 | tf_op jit(solution)/shard_map/all_gather | solution.py:52
  185.7 28.6 %all-gather.8 = f32[8,1,8192]{2,1,0:T(1,128)S(1)} all-gather(f32[1,1,8192]{2,1,0:T(1,128)S(1)} %bitcast.323), channel_id=1, replica_groups=mesh['gx_0'=8,'gx_1'=4,'gx_2'=2,'gy'=4] {'gx_0'}, dimensions={0}, use_global_device_ids=true | all-gather | bytes 294912 | tf_op jit(solution)/shard_map/all_gather | solution.py:52
  214.3 24.8 %all-gather.5 = f32[8,1,8192]{2,1,0:T(1,128)S(1)} all-gather(f32[1,1,8192]{2,1,0:T(1,128)S(1)} %get-tuple-element.8), channel_id=1, replica_groups=mesh['gx_0'=8,'gx_1'=4,'gx_2'=2,'gy'=4] {'gx_0'}, dimensions={0}, use_global_device_ids=true | all-gather | bytes 294912 | tf_op jit(solution)/shard_map/all_gather | solution.py:52
  239.1 0.4 fusion.18
  239.5 0.4 multiply_add_fusion.7
  240.1 0.6 multiply_add_fusion.6
  242.6 2.0 all-gather.9
  244.9 12.4 %all-gather.10 = f32[4,2,8192]{2,1,0:T(2,128)S(1)} all-gather(f32[1,2,8192]{2,1,0:T(2,128)S(1)} %maximum_bitcast_fusion.1), channel_id=3, replica_groups=mesh['gx_0'=8,'gx_1'=4,'gx_2'=2,'gy'=4] {'gx_1'}, dimensions={0}, use_global_device_ids=true | all-gather | bytes 327680 | tf_op jit(solution)/shard_map/all_gather | solution.py:70
  257.7 25.5 %all-gather.11 = f32[8,2,8192]{2,1,0:T(2,128)S(1)} all-gather(f32[1,2,8192]{2,1,0:T(2,128)S(1)} %maximum_bitcast_fusion.2), channel_id=4, replica_groups=mesh['gx_0'=8,'gx_1'=4,'gx_2'=2,'gy'=4] {'gx_0'}, dimensions={0}, use_global_device_ids=true | all-gather | bytes 589824 | tf_op jit(solution)/shard_map/all_gather | solution.py:70
  283.2 0.3 broadcast_select_fusion.1
  283.9 2.5 copy.14
  (56 shorter events, 5.8 us)
Async XLA Ops:
  1.6 5.9 %collective-permute-start.1 = (f32[3,16,512]{2,1,0:T(8,128)S(1)}, f32[3,16,512]{2,1,0:T(8,128)S(1)}, u32[]{:S(2)}, u32[]{:S(2)}) collective-permute-start(f32[3,16,512]{2,1,0:T(8,128)S(1)} %get-tuple-element.17), channel_id=1, source_target_pairs={{0,4},{4,8},{8,12},{12,16},{16,20},{20,24},{24,28},{28,32},{32,36}... | collective-permute-start | bytes 294920 | tf_op jit(solution)/shard_map/ppermute | solution.py:23
  3.5 6.3 %collective-permute-start = (f32[3,16,512]{2,1,0:T(8,128)S(1)}, f32[3,16,512]{2,1,0:T(8,128)S(1)}, u32[]{:S(2)}, u32[]{:S(2)}) collective-permute-start(f32[3,16,512]{2,1,0:T(8,128)S(1)} %get-tuple-element.16), channel_id=1, source_target_pairs={{4,0},{8,4},{12,8},{16,12},{20,16},{24,20},{28,24},{32,28},{36,32}... | collective-permute-start | bytes 294920 | tf_op jit(solution)/shard_map/ppermute | solution.py:24
  7.5 2.3 copy-start.1
  7.5 2.8 copy-start.4
  45.0 5.8 %copy-start.5 = (f32[16,512]{1,0:T(8,128)S(1)}, f32[16,512]{1,0:T(8,128)}, u32[]{:S(2)}) copy-start(f32[16,512]{1,0:T(8,128)} %param.5) | copy-start | bytes 98308
  45.0 100.8 %all-to-all-start = ((f32[4,512,1024]{2,1,0:T(8,128)}), f32[4,512,1024]{2,1,0:T(8,128)}, u32[]{:S(2)}, u32[]{:S(2)}) async-start(f32[4,512,1024]{2,1,0:T(8,128)} %fusion.4), calls=%async_computation | async-start | bytes 16777216 | tf_op jit(solution)/shard_map/all_to_all | solution.py:37
  153.6 2.0 copy-start
  156.2 1.6 copy-start.3
  242.5 41.2 %copy-start.2 = (f32[64,8192]{1,0:T(8,128)S(1)}, f32[64,8192]{1,0:T(8,128)}, u32[]{:S(2)}) copy-start(f32[64,8192]{1,0:T(8,128)} %rev.3) | copy-start | bytes 6291460
where the time goes:
time: 287 us; the launch traced here: 286 us
  blocking collectives  121 us (42%)
  waiting for transfers between devices  72.3 us (25%)
  local copies, waits for them, and re-layouts  33.5 us (12%)
  matrix products  31.3 us (11%)
  other arithmetic  15.4 us (5%)
  starting transfers between devices  11.3 us (4%)
    all_gather x6, blocking collectives, carried_in(): pieces = jax.tree.map(lambda part: lax.all_gather(part, axis), so_far)  81.5 us
    all_to_all x1, waiting for transfers between devices, sum_at_owner(): lax.all_to_all(parts, axis, split_axis=0, concat_axis=0, tiled=True)  71.9 us
    all_gather x3, blocking collectives, all_in_one(): both, at, found = (lax.all_gather(jnp.concatenate(lines), axis), 0, {})  39.9 us
    dot_general x1, matrix products, body(): lax.dot_general(table, source, (((0,), (1,)), ((), ())), precision=highes...  31.3 us
    rev x1, local copies, waits for them, and re-layouts, body(): pressure = local_back + powers[::-1] * after[1][None, :]  20 us
    unnamed x20, local copies, waits for them, and re-layouts  7.56 us
    reduce_sum x1, other arithmetic, sum_at_owner(): return arrived.sum(axis=0)  5.88 us
    all_to_all x1, starting transfers between devices, sum_at_owner(): lax.all_to_all(parts, axis, split_axis=0, concat_axis=0, tiled=True)  5.77 us
  transfers between devices with their start and end apart: 3, of which 2 were waited for; matrix products, arithmetic and copies ran while one was open for 8% of the time, Pallas kernels for 0%

commit v1 on v0

v1 whole, which is shorter than its diff:
```python
import functools
import math

import jax
import jax.numpy as jnp
import ml_dtypes
import numpy as np
from jax import lax
from jax.experimental import pallas as pl
from jax.experimental.pallas import tpu as pltpu
from jax.sharding import PartitionSpec as P

MESH = pl.DeviceIdType.MESH
NY = 2048
GY = 4
CELLS = 64
PLANES = 16
COLS = 512
OWN = CELLS // GY
ROUNDS = (1, 2, 0, 3)
STEP = OWN // len(ROUNDS)
F32 = jnp.float32
BF16 = jnp.bfloat16


@functools.cache
def cosine_tables():
    n = np.arange(NY, dtype=np.int64)
    phase = (2 * n[:, None] + 1) * n[None, :] % (4 * NY)
    table = math.sqrt(2.0 / NY) * np.cos(np.pi * phase.astype(np.float64) / (2.0 * NY))
    high = table.astype(ml_dtypes.bfloat16)
    low = (table - high.astype(np.float64)).astype(ml_dtypes.bfloat16)
    return high, low


def split(value):
    high = value.astype(BF16)
    return high, (value - high.astype(F32)).astype(BF16)


def responses(damping):
    power, gain = damping * damping, damping
    for s in range(9):
        gain = gain * (1.0 + power)
        if s == 5:
            block = gain
            power = power * power
            block_scale = None
        else:
            power = power * power
    scale = damping
    for _ in range(6):
        scale = scale * scale
    block_scale = scale
    for _ in range(3):
        scale = scale * scale
    return block_scale, scale, block, gain


def kernel(
    u, w, damping, high_hbm, low_hbm,
    second_out, coeffs_out, pressure_out,
    source, second, rows, modes, coeffs, forward, table_hi, table_lo, lhs,
    halo, lines, gathered, slabs, back, carried, small,
    halo_send, halo_recv, row_send, row_recv, mode_send, mode_recv,
    a_send, a_recv, b_send, b_recv, c_send, c_recv, table_sem, out_sem,
):
    gx, gy = lax.axis_index("gx"), lax.axis_index("gy")
    z, member = gx // 8, lax.rem(gx, 8)

    def over_gy(d):
        return {"gy": lax.rem(gy + d, GY)}

    def in_slab(d):
        return {"gx": z * 8 + lax.rem(member + d, 8)}

    def over_z(d):
        return {"gx": lax.rem(z + d, 8) * 8 + member}

    following, previous = {"gx": lax.rem(gx + 1, 64)}, {"gx": lax.rem(gx + 63, 64)}
    peers = [following, previous] + [over_gy(d) for d in range(1, GY)]
    peers += [in_slab(d) for d in range(1, 8)] + [over_z(d) for d in range(1, 8)]
    barrier = pltpu.get_barrier_semaphore()
    for peer in peers:
        pl.semaphore_signal(barrier, inc=1, device_id=peer, device_id_type=MESH)

    tables = []
    for d in range(GY):
        block = pl.ds(pl.multiple_of(lax.rem(gy + GY - d, GY) * COLS, COLS), COLS)
        here = pl.ds(d * COLS, COLS)
        tables.append(pltpu.make_async_copy(high_hbm.at[block], table_hi.at[here], table_sem.at[2 * d]))
        tables.append(pltpu.make_async_copy(low_hbm.at[block], table_lo.at[here], table_sem.at[2 * d + 1]))
    for copy in tables:
        copy.start()

    def stencil(at, i):
        m3, m2, m1, c, p1, p2, p3 = [at(k) for k in range(-3, 4)]
        first = 0.75 * (p1 - m1) - 0.15 * (p2 - m2) + (1.0 / 60.0) * (p3 - m3)
        source[i] = first + w[i]
        second[i] = 1.5 * (p1 + m1) - 0.15 * (p2 + m2) + (1.0 / 90.0) * (p3 + m3) - (49.0 / 18.0) * c

    def inside(i, carry):
        stencil(lambda k: u[i + k], i)
        return carry

    lax.fori_loop(3, CELLS - 3, inside, 0)

    pl.semaphore_wait(barrier, len(peers))

    def remote(src, dst, send, recv, peer):
        return pltpu.make_async_remote_copy(
            src_ref=src, dst_ref=dst, send_sem=send, recv_sem=recv, device_id=peer, device_id_type=MESH
        )

    halos = [
        remote(u.at[pl.ds(CELLS - 3, 3)], halo.at[0], halo_send.at[0], halo_recv.at[0], following),
        remote(u.at[pl.ds(0, 3)], halo.at[1], halo_send.at[1], halo_recv.at[1], previous),
    ]
    for copy in halos:
        copy.start()

    row_copies, mode_copies = {}, {}

    def send_rows(q):
        for d in range(1, GY):
            start = lax.rem(gy + d, GY) * OWN + q * STEP
            k = (d - 1) * len(ROUNDS) + q
            row_copies[d, q] = remote(
                source.at[pl.ds(start, STEP)], rows.at[d - 1, pl.ds(q * STEP, STEP)],
                row_send.at[k], row_recv.at[k], over_gy(d),
            )
            row_copies[d, q].start()

    send_rows(ROUNDS[0])
    send_rows(ROUNDS[1])
    for copy in halos:
        copy.wait()
    low_edge, high_edge = (gx > 0).astype(F32), (gx < 63).astype(F32)

    def edge(i):
        def at(k):
            j = i + k
            if j < 0:
                return halo[0, j + 3] * low_edge
            if j >= CELLS:
                return halo[1, j - CELLS] * high_edge
            return u[j]

        stencil(at, i)

    for i in (0, 1, 2, CELLS - 3, CELLS - 2, CELLS - 1):
        edge(i)
    send_rows(ROUNDS[2])
    send_rows(ROUNDS[3])
    second_copy = pltpu.make_async_copy(second, second_out, out_sem.at[0])
    second_copy.start()
    for copy in tables:
        copy.wait()

    height = STEP * PLANES

    def transform(q):
        for d in range(GY):
            if d:
                row_copies[d, q].wait_recv()
                part = rows[d - 1, q * STEP : (q + 1) * STEP]
            else:
                part = source[pl.ds(gy * OWN + q * STEP, STEP)]
            hi, lo = split(part.reshape(height, COLS))
            lhs[:height, d * COLS : (d + 1) * COLS] = hi
            lhs[height:, d * COLS : (d + 1) * COLS] = lo

        def columns(j, carry):
            at = pl.ds(pl.multiple_of(j * 256, 256), 256)
            both = jnp.dot(lhs[...], table_hi[:, at], preferred_element_type=F32)
            cross = jnp.dot(lhs[:height], table_lo[:, at], preferred_element_type=F32)
            total = both[:height] + both[height:] + cross
            modes[j // 2, q * STEP : (q + 1) * STEP, :, pl.ds(pl.multiple_of(lax.rem(j, 2) * 256, 256), 256)] = (
                total.reshape(STEP, PLANES, 256)
            )
            return carry

        lax.fori_loop(0, NY // 256, columns, 0)
        for d in range(1, GY):
            k = (d - 1) * len(ROUNDS) + q
            mode_copies[d, q] = remote(
                modes.at[lax.rem(gy + d, GY), pl.ds(q * STEP, STEP)],
                coeffs.at[pl.ds(gy * OWN + q * STEP, STEP)],
                mode_send.at[k], mode_recv.at[k], over_gy(d),
            )
            mode_copies[d, q].start()
        coeffs[pl.ds(gy * OWN + q * STEP, STEP)] = modes[gy, q * STEP : (q + 1) * STEP]

    for q in ROUNDS:
        transform(q)

    for q in ROUNDS:
        for d in range(1, GY):
            mode_copies[d, q].wait_recv()
    coeffs_copy = pltpu.make_async_copy(coeffs, coeffs_out, out_sem.at[1])
    coeffs_copy.start()

    lam = damping[...]
    v = (1.0 - lam) * (1.0 + lam)
    weight = v * jnp.sqrt(v)

    def ahead(i, value):
        value = weight * coeffs[i] + lam * value
        forward[i] = value
        return value

    def behind(i, value):
        return forward[CELLS - 1 - i] + lam * value

    zero = jnp.zeros((PLANES, COLS), F32)
    end = lax.fori_loop(0, CELLS, ahead, zero, unroll=4)
    start = lax.fori_loop(0, CELLS, behind, zero, unroll=4)

    def groups():
        for g in range(8):
            yield g, slice(8 * (g // 4), 8 * (g // 4) + 8), slice(128 * (g % 4), 128 * (g % 4) + 128)

    for g, sub, lane in groups():
        lines[g, 0] = end[sub, lane]
        lines[g, 1] = start[sub, lane]
        small[g] = lam[sub, lane]

    a_copies = []
    for d in range(1, 8):
        copy = remote(lines.at[lax.rem(member + d, 8)], gathered.at[member], a_send.at[d - 1], a_recv.at[d - 1], in_slab(d))
        copy.start()
        a_copies.append(copy)
    gathered[member] = lines[member]
    scale, slab_scale, answer, slab_answer = responses(small[member])
    for copy in a_copies:
        copy.wait()
    s_slab = jnp.zeros((8, 128), F32)
    seen = []
    for m in range(8):
        seen.append(s_slab)
        s_slab = scale * s_slab + gathered[m, 0]
    t_slab = jnp.zeros((8, 128), F32)
    for m in reversed(range(8)):
        t_slab = gathered[m, 1] + answer * seen[m] + scale * t_slab
    slabs[z, 0] = s_slab
    slabs[z, 1] = t_slab
    b_copies = []
    for d in range(1, 8):
        copy = remote(slabs.at[z], slabs.at[z], b_send.at[d - 1], b_recv.at[d - 1], over_z(d))
        copy.start()
        b_copies.append(copy)
    for copy in b_copies:
        copy.wait()
    f = jnp.zeros((8, 128), F32)
    seen = []
    for k in range(8):
        seen.append(f)
        small[8 + k] = f
        f = slab_scale * f + slabs[k, 0]
    p = jnp.zeros((8, 128), F32)
    for k in reversed(range(8)):
        small[16 + k] = p
        p = slabs[k, 1] + slab_answer * seen[k] + slab_scale * p
    f, p = small[8 + z], small[16 + z]
    seen = []
    for m in range(8):
        seen.append(f)
        back[m, 0] = f
        f = scale * f + gathered[m, 0]
    for m in reversed(range(8)):
        back[m, 1] = p
        p = gathered[m, 1] + answer * seen[m] + scale * p
    c_copies = []
    for d in range(1, 8):
        copy = remote(back.at[lax.rem(member + d, 8)], carried.at[member], c_send.at[d - 1], c_recv.at[d - 1], in_slab(d))
        copy.start()
        c_copies.append(copy)
    carried[member] = back[member]
    for copy in c_copies:
        copy.wait()

    def joined(which):
        halves = [jnp.concatenate([carried[4 * h + g, which] for g in range(4)], axis=1) for h in range(2)]
        return jnp.concatenate(halves, axis=0)

    lax.fori_loop(0, CELLS, ahead, joined(0), unroll=4)
    second_copy.wait()

    def final(i, value):
        k = CELLS - 1 - i
        value = forward[k] + lam * value
        second[k] = value
        return value

    lax.fori_loop(0, CELLS, final, joined(1), unroll=4)
    pressure_copy = pltpu.make_async_copy(second, pressure_out, out_sem.at[2])
    pressure_copy.start()
    for q in ROUNDS:
        for d in range(1, GY):
            row_copies[d, q].wait_send()
            mode_copies[d, q].wait_send()
    coeffs_copy.wait()
    pressure_copy.wait()


def body(velocity_u, wall_strain, damping):
    high, low = cosine_tables()
    block = (CELLS, PLANES, COLS)
    vmem = pl.BlockSpec(memory_space=pltpu.VMEM)
    anywhere = pl.BlockSpec(memory_space=pl.ANY)
    dma = pltpu.SemaphoreType.DMA
    n = 3 * len(ROUNDS)
    return pl.pallas_call(
        kernel,
        out_shape=[jax.ShapeDtypeStruct(block, F32)] * 3,
        in_specs=[vmem, vmem, vmem, anywhere, anywhere],
        out_specs=[anywhere] * 3,
        scratch_shapes=[
            pltpu.VMEM(block, F32),
            pltpu.VMEM(block, F32),
            pltpu.VMEM((GY - 1, OWN, PLANES, COLS), F32),
            pltpu.VMEM((GY, OWN, PLANES, COLS), F32),
            pltpu.VMEM(block, F32),
            pltpu.VMEM(block, F32),
            pltpu.VMEM((NY, NY), BF16),
            pltpu.VMEM((NY, NY), BF16),
            pltpu.VMEM((2 * STEP * PLANES, NY), BF16),
            pltpu.VMEM((2, 3, PLANES, COLS), F32),
            pltpu.VMEM((8, 2, 8, 128), F32),
            pltpu.VMEM((8, 2, 8, 128), F32),
            pltpu.VMEM((8, 2, 8, 128), F32),
            pltpu.VMEM((8, 2, 8, 128), F32),
            pltpu.VMEM((8, 2, 8, 128), F32),
            pltpu.VMEM((24, 8, 128), F32),
            dma((2,)), dma((2,)), dma((n,)), dma((n,)), dma((n,)), dma((n,)),
            dma((7,)), dma((7,)), dma((7,)), dma((7,)), dma((7,)), dma((7,)),
            dma((8,)), dma((3,)),
        ],
        compiler_params=pltpu.CompilerParams(
            collective_id=0, has_side_effects=True, vmem_limit_bytes=56 << 20
        ),
        name="channel",
    )(velocity_u, wall_strain, damping, jnp.asarray(high), jnp.asarray(low))


def solution(mesh):
    spec = P("gx", None, "gy")
    return jax.shard_map(
        body,
        mesh=mesh,
        in_specs=(spec, spec, P(None, "gy")),
        out_specs=(spec, spec, spec),
        check_vma=False,
    )
```

time: 287 us -> 83.4 us (0.29)
  the two profiles are of different devices: /device:TPU:8 before, /device:TPU:1 now
where the time goes in v1:
time: 83.4 us; the launch traced here: 83.2 us
  Pallas kernels  75.5 us (91%)
  local copies, waits for them, and re-layouts  7.04 us (8%)
    pallas_call x1, Pallas kernels, body(): pl.pallas_call(kernel, out_shape=[jax.ShapeDtypeStruct(block, F32)] * 3,...  75.5 us
    unnamed x7, local copies, waits for them, and re-layouts  7.04 us

profile of v1, /device:TPU:1, one launch (start us, length us, event | category | flops | bytes accessed | tf_op | source)
XLA Modules:
  0.0 83.2 jit_solution(18011170642288419551)
XLA Ops:
  0.6 75.5 %channel.1 = (f32[64,16,512]{2,1,0:T(8,128)}, f32[64,16,512]{2,1,0:T(8,128)}, f32[64,16,512]{2,1,0:T(8,128)}) custom-call(f32[64,16,512]{2,1,0:T(8,128)} %u.1, f32[64,16,512]{2,1,0:T(8,128)} %w.1, f32[16,512]{1,0:T(8,128)} %damping.1, bf16[2048,2048]{1,0:T(8,128)(2,1)} %constant.4.clone.high_hbm, bf16[2048,2048]{1,0:T(8,128)(2,1)} %constant.5.clone.low_hbm), custom_call_target="tpu_custom_call" | custom-call | tf_op jit(solution)/shard_map/channel/pallas_call | solution.py:313
  76.2 0.0 copy-start.1
  76.2 3.4 %copy.11 = f32[64,16,512]{2,1,0:T(8,128)} copy(f32[64,16,512]{2,1,0:T(8,128)} %get-tuple-element.6) | data formatting | bytes 4194304
  79.6 0.0 copy-done.1
  79.6 0.0 copy-start
  79.6 1.3 %copy.12 = f32[64,16,512]{2,1,0:T(8,128)} copy(f32[64,16,512]{2,1,0:T(8,128)S(1)} %copy-done.1) | data formatting | bytes 4194304
  80.9 1.0 %copy-done = f32[64,16,512]{2,1,0:T(8,128)S(1)} copy-done((f32[64,16,512]{2,1,0:T(8,128)S(1)}, f32[64,16,512]{2,1,0:T(8,128)}, u32[]{:S(2)}) %copy-start) | copy-done | bytes 2097176
  81.9 1.3 %copy.13 = f32[64,16,512]{2,1,0:T(8,128)} copy(f32[64,16,512]{2,1,0:T(8,128)S(1)} %copy-done) | data formatting | bytes 4194304
Async XLA Ops:
  76.2 3.4 %copy-start.1 = (f32[64,16,512]{2,1,0:T(8,128)S(1)}, f32[64,16,512]{2,1,0:T(8,128)}, u32[]{:S(2)}) copy-start(f32[64,16,512]{2,1,0:T(8,128)} %get-tuple-element.7) | copy-start | bytes 6291460
  79.6 2.3 %copy-start = (f32[64,16,512]{2,1,0:T(8,128)S(1)}, f32[64,16,512]{2,1,0:T(8,128)}, u32[]{:S(2)}) copy-start(f32[64,16,512]{2,1,0:T(8,128)} %get-tuple-element.8) | copy-start | bytes 6291460

commit v2 on v1

v2 whole, which is shorter than its diff:
```python
import functools
import math

import jax
import jax.numpy as jnp
import ml_dtypes
import numpy as np
from jax import lax
from jax.experimental import pallas as pl
from jax.experimental.pallas import tpu as pltpu
from jax.sharding import PartitionSpec as P

MESH = pl.DeviceIdType.MESH
NY = 2048
GY = 4
CELLS = 64
PLANES = 16
COLS = 512
HALF = COLS // 2
OWN = CELLS // GY
ROUNDS = (1, 2, 0, 3)
STEP = OWN // len(ROUNDS)
PIECE = STEP // 2
F32 = jnp.float32
BF16 = jnp.bfloat16


@functools.cache
def cosine_tables():
    n = np.arange(NY, dtype=np.int64)
    phase = (2 * n[:, None] + 1) * n[None, :] % (4 * NY)
    table = math.sqrt(2.0 / NY) * np.cos(np.pi * phase.astype(np.float64) / (2.0 * NY))
    high = table.astype(ml_dtypes.bfloat16)
    low = (table - high.astype(np.float64)).astype(ml_dtypes.bfloat16)
    return high, low


def split(value):
    high = value.astype(BF16)
    return high, (value - high.astype(F32)).astype(BF16)


def response(damping, doublings):
    power, gain = damping * damping, damping * (1.0 + damping * damping)
    for _ in range(doublings - 1):
        power = power * power
        gain = gain * (1.0 + power)
    scale = damping
    for _ in range(doublings):
        scale = scale * scale
    return scale, gain


def weight_of(damping):
    v = (1.0 - damping) * (1.0 + damping)
    return v * jnp.sqrt(v)


def kernel(
    u_hbm, w_hbm, damping_hbm, high_hbm, low_hbm,
    second, coeffs, factors, carried,
    u, w, damping, source, rows, modes, table_hi, table_lo, lhs,
    halo, late_damping, partial, arrived, lines, gathered, slabs, back, small,
    load_sem, table_sem, halo_send, halo_recv, damp_send, damp_recv, row_send, row_recv,
    early_send, early_recv, late_send, late_recv, part_send, part_recv,
    a_send, a_recv, b_send, b_recv, c_send, c_recv,
):
    gx, gy = lax.axis_index("gx"), lax.axis_index("gy")
    z, member = gx // 8, lax.rem(gx, 8)

    def over_gy(d):
        return {"gy": lax.rem(gy + d, GY)}

    def in_slab(d):
        return {"gx": z * 8 + lax.rem(member + d, 8)}

    def over_z(d):
        return {"gx": lax.rem(z + d, 8) * 8 + member}

    following, previous = {"gx": lax.rem(gx + 1, 64)}, {"gx": lax.rem(gx + 63, 64)}
    peers = [following, previous] + [over_gy(d) for d in range(1, GY)]
    peers += [in_slab(d) for d in range(1, 8)] + [over_z(d) for d in range(1, 8)]
    barrier = pltpu.get_barrier_semaphore()
    for peer in peers:
        pl.semaphore_signal(barrier, inc=1, device_id=peer, device_id_type=MESH)

    loads = [
        pltpu.make_async_copy(u_hbm, u, load_sem.at[0]),
        pltpu.make_async_copy(w_hbm, w, load_sem.at[1]),
        pltpu.make_async_copy(damping_hbm, damping, load_sem.at[2]),
    ]
    tables = []
    for d in range(GY):
        block = pl.ds(pl.multiple_of(lax.rem(gy + GY - d, GY) * COLS, COLS), COLS)
        here = pl.ds(d * COLS, COLS)
        tables.append(pltpu.make_async_copy(high_hbm.at[block], table_hi.at[here], table_sem.at[2 * d]))
        tables.append(pltpu.make_async_copy(low_hbm.at[block], table_lo.at[here], table_sem.at[2 * d + 1]))
    for copy in loads + tables:
        copy.start()

    def remote(src, dst, send, recv, peer):
        return pltpu.make_async_remote_copy(
            src_ref=src, dst_ref=dst, send_sem=send, recv_sem=recv, device_id=peer, device_id_type=MESH
        )

    def stencil(at, i):
        m3, m2, m1, c, p1, p2, p3 = [at(k) for k in range(-3, 4)]
        first = 0.75 * (p1 - m1) - 0.15 * (p2 - m2) + (1.0 / 60.0) * (p3 - m3)
        source[i] = first + w[i]
        second[i] = 1.5 * (p1 + m1) - 0.15 * (p2 + m2) + (1.0 / 90.0) * (p3 + m3) - (49.0 / 18.0) * c

    def inside(first, last):
        def step(i, carry):
            stencil(lambda k: u[i + k], i)
            return carry

        lax.fori_loop(first, last, step, 0)

    def inner_chunk(q):
        for j in range(GY):
            inside(max(j * OWN + q * STEP, 3), min(j * OWN + q * STEP + STEP, CELLS - 3))

    row_copies, early_copies, late_copies = {}, {}, {}

    def send_rows(q):
        for half in range(2):
            at = q * STEP + half * PIECE
            for d in range(1, GY):
                k = ((d - 1) * len(ROUNDS) + q) * 2 + half
                copy = remote(
                    source.at[pl.ds(lax.rem(gy + d, GY) * OWN + at, PIECE)], rows.at[d - 1, pl.ds(at, PIECE)],
                    row_send.at[k], row_recv.at[k], over_gy(d),
                )
                copy.start()
                row_copies[d, q, half] = copy

    loads[0].wait()
    loads[1].wait()
    loads[2].wait()
    inner_chunk(ROUNDS[0])
    pl.semaphore_wait(barrier, len(peers))
    halos = [
        remote(u.at[pl.ds(CELLS - 3, 3)], halo.at[0], halo_send.at[0], halo_recv.at[0], following),
        remote(u.at[pl.ds(0, 3)], halo.at[1], halo_send.at[1], halo_recv.at[1], previous),
    ]
    for copy in halos:
        copy.start()
    send_rows(ROUNDS[0])
    inner_chunk(ROUNDS[1])
    send_rows(ROUNDS[1])
    damps = []
    for d in range(1, GY):
        copy = remote(
            damping.at[:, pl.ds(HALF, HALF)], late_damping.at[gy], damp_send.at[d - 1], damp_recv.at[d - 1], over_gy(d)
        )
        copy.start()
        damps.append(copy)
    late_damping[gy] = damping[:, HALF:]
    inner_chunk(ROUNDS[2])
    inner_chunk(ROUNDS[3])
    for copy in halos:
        copy.wait()
    low_edge, high_edge = (gx > 0).astype(F32), (gx < 63).astype(F32)

    def edge(i):
        def at(k):
            j = i + k
            if j < 0:
                return halo[0, j + 3] * low_edge
            if j >= CELLS:
                return halo[1, j - CELLS] * high_edge
            return u[j]

        stencil(at, i)

    for i in (0, 1, 2):
        edge(i)
    send_rows(ROUNDS[2])
    for i in (CELLS - 3, CELLS - 2, CELLS - 1):
        edge(i)
    send_rows(ROUNDS[3])

    lam = damping[...]
    factors[0] = lam
    factors[1] = weight_of(lam)
    for g in range(8):
        small[g] = lam[8 * (g // 4) : 8 * (g // 4) + 8, 128 * (g % 4) : 128 * (g % 4) + 128]
    scale, answer = response(small[member], 6)
    slab_scale, slab_answer = response(small[member], 9)
    sub_scale, sub_answer = response(lam[:, HALF:], 4)
    for copy in tables:
        copy.wait()

    height = STEP * PLANES

    def send_modes(q, late):
        copies, send, recv = (late_copies, late_send, late_recv) if late else (early_copies, early_send, early_recv)
        lanes = pl.ds(HALF if late else 0, HALF)
        for d in range(1, GY):
            k = (d - 1) * len(ROUNDS) + q
            copy = remote(
                modes.at[lax.rem(gy + d, GY), pl.ds(q * STEP, STEP), :, lanes],
                coeffs.at[pl.ds(gy * OWN + q * STEP, STEP), :, lanes],
                send.at[k], recv.at[k], over_gy(d),
            )
            copy.start()
            copies[d, q] = copy

    def transform(q):
        for d in range(GY):
            if d:
                row_copies[d, q, 0].wait_recv()
                row_copies[d, q, 1].wait_recv()
                part = rows[d - 1, q * STEP : (q + 1) * STEP]
            else:
                part = source[pl.ds(gy * OWN + q * STEP, STEP)]
            hi, lo = split(part.reshape(height, COLS))
            lhs[:height, d * COLS : (d + 1) * COLS] = hi
            lhs[height:, d * COLS : (d + 1) * COLS] = lo

        def columns(j, carry):
            at = pl.ds(pl.multiple_of(j * 256, 256), 256)
            both = jnp.dot(lhs[...], table_hi[:, at], preferred_element_type=F32)
            cross = jnp.dot(lhs[:height], table_lo[:, at], preferred_element_type=F32)
            total = both[:height] + both[height:] + cross
            modes[j // 2, q * STEP : (q + 1) * STEP, :, pl.ds(pl.multiple_of(lax.rem(j, 2) * 256, 256), 256)] = (
                total.reshape(STEP, PLANES, 256)
            )
            return carry

        lax.fori_loop(0, NY // 256, columns, 0, unroll=2)
        send_modes(q, False)
        coeffs[pl.ds(gy * OWN + q * STEP, STEP)] = modes[gy, q * STEP : (q + 1) * STEP]

    for q in ROUNDS:
        transform(q)

    for copy in damps:
        copy.wait()
    late = [late_damping[o] for o in range(GY)]
    late_weight = [weight_of(x) for x in late]
    blank = jnp.zeros((PLANES, HALF), F32)

    def own_rows(i, carry):
        found = []
        for o, (s, t, power) in enumerate(carry):
            s = late_weight[o] * modes[o, i, :, HALF:] + late[o] * s
            found.append((s, t + power * s, power * late[o]))
        return tuple(found)

    sums = lax.fori_loop(0, OWN, own_rows, ((blank, blank, blank + 1.0),) * GY)
    for o in range(GY):
        partial[o, 0] = sums[o][0]
        partial[o, 1] = sums[o][1]
    parts = []
    for d in range(1, GY):
        copy = remote(partial.at[lax.rem(gy + d, GY)], arrived.at[gy], part_send.at[d - 1], part_recv.at[d - 1], over_gy(d))
        copy.start()
        parts.append(copy)
    arrived[gy] = partial[gy]
    send_modes(ROUNDS[0], True)
    send_modes(ROUNDS[1], True)

    for q in ROUNDS:
        for d in range(1, GY):
            early_copies[d, q].wait_recv()
    first, first_weight = lam[:, :HALF], factors[1, :, :HALF]

    def all_rows(i, carry):
        s, t, power = carry
        s = first_weight * coeffs[i, :, :HALF] + first * s
        return s, t + power * s, power * first

    s_early, t_early, _ = lax.fori_loop(0, CELLS, all_rows, (blank, blank, blank + 1.0), unroll=4)
    for copy in parts:
        copy.wait()
    s_late, seen = blank, []
    for j in range(GY):
        seen.append(s_late)
        s_late = sub_scale * s_late + arrived[j, 0]
    t_late = blank
    for j in reversed(range(GY)):
        t_late = arrived[j, 1] + sub_answer * seen[j] + sub_scale * t_late
    for h in range(2):
        sub = slice(8 * h, 8 * h + 8)
        for g in range(2):
            lane = slice(128 * g, 128 * g + 128)
            lines[4 * h + g, 0] = s_early[sub, lane]
            lines[4 * h + g, 1] = t_early[sub, lane]
            lines[4 * h + 2 + g, 0] = s_late[sub, lane]
            lines[4 * h + 2 + g, 1] = t_late[sub, lane]

    a_copies = []
    for d in range(1, 8):
        copy = remote(lines.at[lax.rem(member + d, 8)], gathered.at[member], a_send.at[d - 1], a_recv.at[d - 1], in_slab(d))
        copy.start()
        a_copies.append(copy)
    gathered[member] = lines[member]
    send_modes(ROUNDS[2], True)
    for copy in a_copies:
        copy.wait()
    tile = jnp.zeros((8, 128), F32)
    s_slab, seen = tile, []
    for m in range(8):
        seen.append(s_slab)
        s_slab = scale * s_slab + gathered[m, 0]
    t_slab = tile
    for m in reversed(range(8)):
        t_slab = gathered[m, 1] + answer * seen[m] + scale * t_slab
    slabs[z, 0] = s_slab
    slabs[z, 1] = t_slab
    b_copies = []
    for d in range(1, 8):
        copy = remote(slabs.at[z], slabs.at[z], b_send.at[d - 1], b_recv.at[d - 1], over_z(d))
        copy.start()
        b_copies.append(copy)
    send_modes(ROUNDS[3], True)
    for copy in b_copies:
        copy.wait()
    f, seen = tile, []
    for k in range(8):
        seen.append(f)
        small[8 + k] = f
        f = slab_scale * f + slabs[k, 0]
    p = tile
    for k in reversed(range(8)):
        small[16 + k] = p
        p = slabs[k, 1] + slab_answer * seen[k] + slab_scale * p
    f, p = small[8 + z], small[16 + z]
    seen = []
    for m in range(8):
        seen.append(f)
        back[m, 0] = f
        f = scale * f + gathered[m, 0]
    for m in reversed(range(8)):
        back[m, 1] = p
        p = gathered[m, 1] + answer * seen[m] + scale * p
    c_copies = []
    for d in range(1, 8):
        copy = remote(back.at[lax.rem(member + d, 8)], carried.at[member], c_send.at[d - 1], c_recv.at[d - 1], in_slab(d))
        copy.start()
        c_copies.append(copy)
    carried[member] = back[member]
    for copy in c_copies:
        copy.wait()
    for q in ROUNDS:
        for d in range(1, GY):
            row_copies[d, q, 0].wait_send()
            row_copies[d, q, 1].wait_send()
            early_copies[d, q].wait_send()
            late_copies[d, q].wait()


def finish(second, coeffs, factors, carried, second_out, coeffs_out, pressure_out, forward, pressure, sem):
    whole = [
        pltpu.make_async_copy(coeffs, coeffs_out, sem.at[0]),
        pltpu.make_async_copy(second, second_out, sem.at[1]),
    ]
    for copy in whole:
        copy.start()
    lam, weight = factors[0], factors[1]

    def joined(which):
        halves = [jnp.concatenate([carried[4 * h + g, which] for g in range(4)], axis=1) for h in range(2)]
        return jnp.concatenate(halves, axis=0)

    def ahead(i, value):
        value = weight * coeffs[i] + lam * value
        forward[i] = value
        return value

    lax.fori_loop(0, CELLS, ahead, joined(0), unroll=4)
    value, quarter = joined(1), CELLS // 4
    for part in reversed(range(4)):

        def behind(i, value):
            k = (part + 1) * quarter - 1 - i
            value = forward[k] + lam * value
            pressure[k] = value
            return value

        value = lax.fori_loop(0, quarter, behind, value, unroll=4)
        here = pl.ds(part * quarter, quarter)
        copy = pltpu.make_async_copy(pressure.at[here], pressure_out.at[here], sem.at[2 + part])
        copy.start()
        whole.append(copy)
    for copy in whole:
        copy.wait()


def body(velocity_u, wall_strain, damping):
    high, low = (jnp.asarray(table) for table in cosine_tables())
    block, plane = (CELLS, PLANES, COLS), (PLANES, COLS)
    vmem = pl.BlockSpec(memory_space=pltpu.VMEM)
    anywhere = pl.BlockSpec(memory_space=pltpu.HBM)
    dma = pltpu.SemaphoreType.DMA
    n, groups = 3 * len(ROUNDS), (8, 2, 8, 128)
    between = pl.pallas_call(
        kernel,
        out_shape=[pltpu.VMEM(shape, F32) for shape in (block, block, (2, *plane), groups)],
        in_specs=[anywhere] * 5,
        out_specs=[vmem] * 4,
        scratch_shapes=[
            pltpu.VMEM(block, F32),
            pltpu.VMEM(block, F32),
            pltpu.VMEM(plane, F32),
            pltpu.VMEM(block, F32),
            pltpu.VMEM((GY - 1, OWN, PLANES, COLS), F32),
            pltpu.VMEM((GY, OWN, PLANES, COLS), F32),
            pltpu.VMEM((NY, NY), BF16),
            pltpu.VMEM((NY, NY), BF16),
            pltpu.VMEM((2 * STEP * PLANES, NY), BF16),
            pltpu.VMEM((2, 3, PLANES, COLS), F32),
            pltpu.VMEM((GY, PLANES, HALF), F32),
            pltpu.VMEM((GY, 2, PLANES, HALF), F32),
            pltpu.VMEM((GY, 2, PLANES, HALF), F32),
            pltpu.VMEM(groups, F32),
            pltpu.VMEM(groups, F32),
            pltpu.VMEM(groups, F32),
            pltpu.VMEM(groups, F32),
            pltpu.VMEM((24, 8, 128), F32),
            dma((3,)), dma((8,)), dma((2,)), dma((2,)), dma((3,)), dma((3,)), dma((2 * n,)), dma((2 * n,)),
            dma((n,)), dma((n,)), dma((n,)), dma((n,)), dma((3,)), dma((3,)),
            dma((7,)), dma((7,)), dma((7,)), dma((7,)), dma((7,)), dma((7,)),
        ],
        compiler_params=pltpu.CompilerParams(
            collective_id=0, has_side_effects=True, vmem_limit_bytes=40 << 20
        ),
        name="exchange",
    )(*[pltpu.with_memory_space_constraint(x, pltpu.HBM) for x in (velocity_u, wall_strain, damping, high, low)])
    return pl.pallas_call(
        finish,
        out_shape=[jax.ShapeDtypeStruct(block, F32)] * 3,
        in_specs=[vmem] * 4,
        out_specs=[anywhere] * 3,
        scratch_shapes=[pltpu.VMEM(block, F32), pltpu.VMEM(block, F32), dma((6,))],
        compiler_params=pltpu.CompilerParams(vmem_limit_bytes=16 << 20),
        name="finish",
    )(*between)


def solution(mesh):
    spec = P("gx", None, "gy")
    return jax.shard_map(
        body,
        mesh=mesh,
        in_specs=(spec, spec, P(None, "gy")),
        out_specs=(spec, spec, spec),
        check_vma=False,
    )
```

time: 83.4 us -> 71.8 us (0.86)
  local copies, waits for them, and re-layouts: 7.04 us -> 0 us
  Pallas kernels: 75.5 us -> 71 us
    unnamed x7 -> x0, local copies, waits for them, and re-layouts: 7.04 us -> none
    pallas_call x1 -> x2, Pallas kernels: 75.5 us -> 71 us  [the longest x1 68.3 us: body(): pl.pallas_call(kernel, out_shape=[pltpu.VMEM(shape, F32) for shape in (bl...]
where the time goes in v2:
time: 71.8 us; the launch traced here: 71.7 us
  Pallas kernels  71 us (99%)
    pallas_call x1, Pallas kernels, body(): pl.pallas_call(kernel, out_shape=[pltpu.VMEM(shape, F32) for shape in (bl...  68.3 us
    pallas_call x1, Pallas kernels, body(): pl.pallas_call(finish, out_shape=[jax.ShapeDtypeStruct(block, F32)] * 3,...  2.7 us

profile of v2, /device:TPU:1, one launch (start us, length us, event | category | flops | bytes accessed | tf_op | source)
XLA Modules:
  0.0 71.7 jit_solution(10410582264884475186)
XLA Ops:
  0.6 68.3 %exchange.1 = (f32[64,16,512]{2,1,0:T(8,128)S(1)}, f32[64,16,512]{2,1,0:T(8,128)S(1)}, f32[2,16,512]{2,1,0:T(8,128)S(1)}, f32[8,2,8,128]{3,2,1,0:T(8,128)S(1)}) custom-call(f32[64,16,512]{2,1,0:T(8,128)} %u_hbm.1, f32[64,16,512]{2,1,0:T(8,128)} %w_hbm.1, f32[16,512]{1,0:T(8,128)} %damping_hbm.1, bf16[2048,2048]{1,0:T(8,128)(2,1)} %constant.4.clone.high_hbm, ...), custom_call_target="tpu_custom_call" | custom-call | tf_op jit(solution)/shard_map/exchange/pallas_call | solution.py:398
  69.0 2.7 %finish.1 = (f32[64,16,512]{2,1,0:T(8,128)}, f32[64,16,512]{2,1,0:T(8,128)}, f32[64,16,512]{2,1,0:T(8,128)}) custom-call(f32[64,16,512]{2,1,0:T(8,128)S(1)} %get-tuple-element.7.second, f32[64,16,512]{2,1,0:T(8,128)S(1)} %get-tuple-element.8.coeffs, f32[2,16,512]{2,1,0:T(8,128)S(1)} %get-tuple-element.9.factors, f32[8,2,8,128]{3,2,1,0:T(8,128)S(1)} %get-tuple-element.10.carried), custom_call_target="tpu_custom_call" | custom-call | tf_op jit(solution)/shard_map/finish/pallas_call | solution.py:431

commit v3 on v2

v3 whole, which is shorter than its diff:
```python
import functools
import math

import jax
import jax.numpy as jnp
import ml_dtypes
import numpy as np
from jax import lax
from jax.experimental import pallas as pl
from jax.experimental.pallas import tpu as pltpu
from jax.sharding import PartitionSpec as P

MESH = pl.DeviceIdType.MESH
NY = 2048
GY = 4
CELLS = 64
PLANES = 16
COLS = 512
OWN = CELLS // GY
ROUNDS = (1, 2, 0, 3)
STEP = OWN // len(ROUNDS)
PIECE = STEP // 2
F32 = jnp.float32
BF16 = jnp.bfloat16


@functools.cache
def cosine_tables():
    n = np.arange(NY, dtype=np.int64)
    phase = (2 * n[:, None] + 1) * n[None, :] % (4 * NY)
    table = math.sqrt(2.0 / NY) * np.cos(np.pi * phase.astype(np.float64) / (2.0 * NY))
    high = table.astype(ml_dtypes.bfloat16)
    low = (table - high.astype(np.float64)).astype(ml_dtypes.bfloat16)
    return high, low


def split(value):
    high = value.astype(BF16)
    return high, (value - high.astype(F32)).astype(BF16)


def response(damping, doublings):
    power, gain = damping * damping, damping * (1.0 + damping * damping)
    for _ in range(doublings - 1):
        power = power * power
        gain = gain * (1.0 + power)
    scale = damping
    for _ in range(doublings):
        scale = scale * scale
    return scale, gain


def weight_of(damping):
    v = (1.0 - damping) * (1.0 + damping)
    return v * jnp.sqrt(v)


def kernel(
    u_hbm, w_hbm, damping_hbm, high_hbm, low_hbm,
    second, coeffs, factors, carried,
    u, w, damping, source, rows, modes, table_hi, table_lo, lhs,
    halo, all_damping, all_weight, sub, partial, arrived, lines, gathered, slabs, chain, back, small,
    load_sem, table_sem, halo_send, halo_recv, damp_send, damp_recv, row_send, row_recv, mode_send, mode_recv,
    part_send, part_recv, a_send, a_recv, b_send, b_recv, c_send, c_recv,
):
    gx, gy = lax.axis_index("gx"), lax.axis_index("gy")
    z, member = gx // 8, lax.rem(gx, 8)

    def over_gy(d):
        return {"gy": lax.rem(gy + d, GY)}

    def in_slab(d):
        return {"gx": z * 8 + lax.rem(member + d, 8)}

    above, below = {"gx": lax.rem(gx + 8, 64)}, {"gx": lax.rem(gx + 56, 64)}
    following, previous = {"gx": lax.rem(gx + 1, 64)}, {"gx": lax.rem(gx + 63, 64)}
    out_up, out_down = jnp.logical_and(member == 7, z < 7), jnp.logical_and(member == 0, z > 0)
    barrier = pltpu.get_barrier_semaphore()

    def greet(peer):
        pl.semaphore_signal(barrier, inc=1, device_id=peer, device_id_type=MESH)

    for d in range(1, GY):
        greet(over_gy(d))
    for d in range(1, 8):
        greet(in_slab(d))
    for needed, peer in ((z < 7, above), (z > 0, below), (out_up, following), (out_down, previous)):

        @pl.when(needed)
        def _(peer=peer):
            greet(peer)

    greeted = 10 + (z < 7).astype(jnp.int32) + (z > 0).astype(jnp.int32)
    greeted = greeted + out_up.astype(jnp.int32) + out_down.astype(jnp.int32)

    loads = [
        pltpu.make_async_copy(u_hbm, u, load_sem.at[0]),
        pltpu.make_async_copy(w_hbm, w, load_sem.at[1]),
        pltpu.make_async_copy(damping_hbm, damping, load_sem.at[2]),
    ]
    tables = []
    for d in range(GY):
        block = pl.ds(pl.multiple_of(lax.rem(gy + GY - d, GY) * COLS, COLS), COLS)
        here = pl.ds(d * COLS, COLS)
        tables.append(pltpu.make_async_copy(high_hbm.at[block], table_hi.at[here], table_sem.at[2 * d]))
        tables.append(pltpu.make_async_copy(low_hbm.at[block], table_lo.at[here], table_sem.at[2 * d + 1]))
    for copy in loads:
        copy.start()

    started = []

    def remote(src, dst, send, recv, peer):
        copy = pltpu.make_async_remote_copy(
            src_ref=src, dst_ref=dst, send_sem=send, recv_sem=recv, device_id=peer, device_id_type=MESH
        )
        copy.start()
        started.append(copy)
        return copy

    def stencil(at, i):
        m3, m2, m1, c, p1, p2, p3 = [at(k) for k in range(-3, 4)]
        first = 0.75 * (p1 - m1) - 0.15 * (p2 - m2) + (1.0 / 60.0) * (p3 - m3)
        source[i] = first + w[i]
        second[i] = 1.5 * (p1 + m1) - 0.15 * (p2 + m2) + (1.0 / 90.0) * (p3 + m3) - (49.0 / 18.0) * c

    def inner_chunk(q):
        def step(i, carry):
            stencil(lambda k: u[i + k], i)
            return carry

        for j in range(GY):
            lax.fori_loop(max(j * OWN + q * STEP, 3), min(j * OWN + q * STEP + STEP, CELLS - 3), step, 0)

    row_copies, mode_copies = {}, {}

    def send_rows(q):
        for half in range(2):
            at = q * STEP + half * PIECE
            for d in range(1, GY):
                k = ((d - 1) * len(ROUNDS) + q) * 2 + half
                src = source.at[pl.ds(lax.rem(gy + d, GY) * OWN + at, PIECE)]
                dst = rows.at[d - 1, pl.ds(at, PIECE)]
                row_copies[d, q, half] = remote(src, dst, row_send.at[k], row_recv.at[k], over_gy(d))

    def send_modes(q):
        for half in range(2):
            at = q * STEP + half * PIECE
            for d in range(1, GY):
                k = ((d - 1) * len(ROUNDS) + q) * 2 + half
                src = modes.at[lax.rem(gy + d, GY), pl.ds(at, PIECE)]
                dst = coeffs.at[pl.ds(gy * OWN + at, PIECE)]
                mode_copies[d, q, half] = remote(src, dst, mode_send.at[k], mode_recv.at[k], over_gy(d))

    height = STEP * PLANES

    def transform(q):
        for d in range(GY):
            if d:
                row_copies[d, q, 0].wait_recv()
                row_copies[d, q, 1].wait_recv()
                part = rows[d - 1, q * STEP : (q + 1) * STEP]
            else:
                part = source[pl.ds(gy * OWN + q * STEP, STEP)]
            hi, lo = split(part.reshape(height, COLS))
            lhs[:height, d * COLS : (d + 1) * COLS] = hi
            lhs[height:, d * COLS : (d + 1) * COLS] = lo

        def columns(j, carry):
            at = pl.ds(pl.multiple_of(j * 256, 256), 256)
            both = jnp.dot(lhs[...], table_hi[:, at], preferred_element_type=F32)
            cross = jnp.dot(lhs[:height], table_lo[:, at], preferred_element_type=F32)
            total = both[:height] + both[height:] + cross
            modes[j // 2, q * STEP : (q + 1) * STEP, :, pl.ds(pl.multiple_of(lax.rem(j, 2) * 256, 256), 256)] = (
                total.reshape(STEP, PLANES, 256)
            )
            return carry

        lax.fori_loop(0, NY // 256, columns, 0, unroll=2)
        coeffs[pl.ds(gy * OWN + q * STEP, STEP)] = modes[gy, q * STEP : (q + 1) * STEP]

    r0, r1, r2, r3 = ROUNDS
    loads[0].wait()
    loads[1].wait()
    loads[2].wait()
    for copy in tables:
        copy.start()
    inner_chunk(r0)
    pl.semaphore_wait(barrier, greeted)

    def halo_copy(k):
        src = u.at[pl.ds((CELLS - 3) * (1 - k), 3)]
        peer = (following, previous)[k]
        return pltpu.make_async_remote_copy(
            src_ref=src, dst_ref=halo.at[k], send_sem=halo_send.at[k], recv_sem=halo_recv.at[k],
            device_id=peer, device_id_type=MESH,
        )

    has_next, has_previous = gx < 63, gx > 0

    @pl.when(has_next)
    def _():
        halo_copy(0).start()

    @pl.when(has_previous)
    def _():
        halo_copy(1).start()

    send_rows(r0)
    inner_chunk(r1)
    send_rows(r1)
    damps = [
        remote(damping, all_damping.at[gy], damp_send.at[d - 1], damp_recv.at[d - 1], over_gy(d)) for d in range(1, GY)
    ]
    all_damping[gy] = damping[...]
    inner_chunk(r2)
    inner_chunk(r3)

    @pl.when(has_previous)
    def _():
        halo_copy(0).wait_recv()
        halo_copy(1).wait_send()

    @pl.when(jnp.logical_not(has_previous))
    def _():
        halo[0] = jnp.zeros((3, PLANES, COLS), F32)

    @pl.when(has_next)
    def _():
        halo_copy(1).wait_recv()
        halo_copy(0).wait_send()

    @pl.when(jnp.logical_not(has_next))
    def _():
        halo[1] = jnp.zeros((3, PLANES, COLS), F32)

    def edge(i):
        def at(k):
            j = i + k
            if j < 0:
                return halo[0, j + 3]
            if j >= CELLS:
                return halo[1, j - CELLS]
            return u[j]

        stencil(at, i)

    for i in (0, 1, 2):
        edge(i)
    send_rows(r2)
    for i in (CELLS - 3, CELLS - 2, CELLS - 1):
        edge(i)
    send_rows(r3)

    lam = damping[...]
    factors[0] = lam
    factors[1] = weight_of(lam)
    for g in range(8):
        small[g] = lam[8 * (g // 4) : 8 * (g // 4) + 8, 128 * (g % 4) : 128 * (g % 4) + 128]
    for k, value in enumerate(response(lam, 4)):
        sub[k] = value
    for k, value in enumerate((*response(small[member], 6), *response(small[member], 9))):
        small[8 + k] = value
    for copy in damps:
        copy.wait_recv()
    for o in range(GY):
        all_weight[o] = weight_of(all_damping[o])
    for copy in tables:
        copy.wait()

    transform(r0)
    send_modes(r0)
    transform(r1)
    transform(r2)
    transform(r3)

    blank = jnp.zeros((PLANES, COLS), F32)
    for o in range(GY):

        def own_rows(i, carry, o=o):
            s, t, power = carry
            s = all_weight[o] * modes[o, i] + all_damping[o] * s
            return s, t + power * s, power * all_damping[o]

        s, t, _ = lax.fori_loop(0, OWN, own_rows, (blank, blank, blank + 1.0), unroll=2)
        partial[o, 0] = s
        partial[o, 1] = t
    parts = [
        remote(
            partial.at[lax.rem(gy + d, GY)], arrived.at[gy], part_send.at[d - 1], part_recv.at[d - 1],
            over_gy(d),
        )
        for d in range(1, GY)
    ]
    arrived[gy] = partial[gy]
    send_modes(r1)
    send_modes(r2)

    for copy in parts:
        copy.wait_recv()
    s, seen = blank, []
    for j in range(GY):
        seen.append(s)
        s = sub[0] * s + arrived[j, 0]
    t = blank
    for j in reversed(range(GY)):
        t = arrived[j, 1] + sub[1] * seen[j] + sub[0] * t
    for g in range(8):
        at = slice(8 * (g // 4), 8 * (g // 4) + 8), slice(128 * (g % 4), 128 * (g % 4) + 128)
        lines[g, 0] = s[at]
        lines[g, 1] = t[at]

    a_copies = [
        remote(lines.at[lax.rem(member + d, 8)], gathered.at[member], a_send.at[d - 1], a_recv.at[d - 1], in_slab(d))
        for d in range(1, 8)
    ]
    gathered[member] = lines[member]
    send_modes(r3)
    for copy in a_copies:
        copy.wait_recv()
    scale, answer, slab_scale, slab_answer = [small[8 + k] for k in range(4)]
    tile = jnp.zeros((8, 128), F32)
    s_slab, seen = tile, []
    for m in range(8):
        seen.append(s_slab)
        s_slab = scale * s_slab + gathered[m, 0]
    t_slab = tile
    for m in reversed(range(8)):
        t_slab = gathered[m, 1] + answer * seen[m] + scale * t_slab
    slabs[1] = jnp.zeros((3, 8, 128), F32)

    def up():
        return pltpu.make_async_remote_copy(
            src_ref=slabs.at[0, pl.ds(0, 1)], dst_ref=chain.at[pl.ds(0, 1)], send_sem=b_send.at[0],
            recv_sem=b_recv.at[0], device_id=above, device_id_type=MESH,
        )

    def down():
        return pltpu.make_async_remote_copy(
            src_ref=slabs.at[0, pl.ds(1, 2)], dst_ref=chain.at[pl.ds(1, 2)], send_sem=b_send.at[1],
            recv_sem=b_recv.at[1], device_id=below, device_id_type=MESH,
        )

    def pass_up():
        @pl.when(z > 0)
        def _():
            up().wait_recv()
            slabs[1, 0] = chain[0]

        slabs[0, 0] = s_slab + slab_scale * slabs[1, 0]

        @pl.when(z < 7)
        def _():
            up().start()

    def pass_down():
        @pl.when(z < 7)
        def _():
            down().wait_recv()
            slabs[1, 1] = chain[1]
            slabs[1, 2] = chain[2]

        slabs[0, 1] = t_slab + slab_scale * (slabs[1, 1] + slabs[1, 2] * s_slab)
        slabs[0, 2] = slab_answer + slab_scale * slab_scale * slabs[1, 2]

        @pl.when(z > 0)
        def _():
            down().start()

    @pl.when(z < 4)
    def _():
        pass_up()
        pass_down()

    @pl.when(z >= 4)
    def _():
        pass_down()
        pass_up()

    f = slabs[1, 0]
    p = slabs[1, 1] + slabs[1, 2] * (s_slab + slab_scale * f)
    seen = []
    for m in range(8):
        seen.append(f)
        back[m, 0] = f
        f = scale * f + gathered[m, 0]
    for m in reversed(range(8)):
        back[m, 1] = p
        p = gathered[m, 1] + answer * seen[m] + scale * p
    c_copies = [
        remote(back.at[lax.rem(member + d, 8)], carried.at[member], c_send.at[d - 1], c_recv.at[d - 1], in_slab(d))
        for d in range(1, 8)
    ]
    carried[member] = back[member]
    for copy in c_copies:
        copy.wait_recv()
    for copy in mode_copies.values():
        copy.wait_recv()

    @pl.when(z < 7)
    def _():
        up().wait_send()

    @pl.when(z > 0)
    def _():
        down().wait_send()

    for copy in started:
        copy.wait_send()


def finish(second, coeffs, factors, carried, second_out, coeffs_out, pressure_out, forward, pressure, sem):
    whole = [
        pltpu.make_async_copy(coeffs, coeffs_out, sem.at[0]),
        pltpu.make_async_copy(second, second_out, sem.at[1]),
    ]
    for copy in whole:
        copy.start()
    lam, weight = factors[0], factors[1]

    def joined(which):
        halves = [jnp.concatenate([carried[4 * h + g, which] for g in range(4)], axis=1) for h in range(2)]
        return jnp.concatenate(halves, axis=0)

    def ahead(i, value):
        value = weight * coeffs[i] + lam * value
        forward[i] = value
        return value

    lax.fori_loop(0, CELLS, ahead, joined(0), unroll=4)
    value, quarter = joined(1), CELLS // 4
    for part in reversed(range(4)):

        def behind(i, value):
            k = (part + 1) * quarter - 1 - i
            value = forward[k] + lam * value
            pressure[k] = value
            return value

        value = lax.fori_loop(0, quarter, behind, value, unroll=4)
        here = pl.ds(part * quarter, quarter)
        copy = pltpu.make_async_copy(pressure.at[here], pressure_out.at[here], sem.at[2 + part])
        copy.start()
        whole.append(copy)
    for copy in whole:
        copy.wait()


def body(velocity_u, wall_strain, damping):
    high, low = (jnp.asarray(table) for table in cosine_tables())
    block, plane = (CELLS, PLANES, COLS), (PLANES, COLS)
    vmem = pl.BlockSpec(memory_space=pltpu.VMEM)
    anywhere = pl.BlockSpec(memory_space=pltpu.HBM)
    dma = pltpu.SemaphoreType.DMA
    n, groups = 6 * len(ROUNDS), (8, 2, 8, 128)
    between = pl.pallas_call(
        kernel,
        out_shape=[pltpu.VMEM(shape, F32) for shape in (block, block, (2, *plane), groups)],
        in_specs=[anywhere] * 5,
        out_specs=[vmem] * 4,
        scratch_shapes=[
            pltpu.VMEM(block, F32),
            pltpu.VMEM(block, F32),
            pltpu.VMEM(plane, F32),
            pltpu.VMEM(block, F32),
            pltpu.VMEM((GY - 1, OWN, *plane), F32),
            pltpu.VMEM((GY, OWN, *plane), F32),
            pltpu.VMEM((NY, NY), BF16),
            pltpu.VMEM((NY, NY), BF16),
            pltpu.VMEM((2 * STEP * PLANES, NY), BF16),
            pltpu.VMEM((2, 3, *plane), F32),
            pltpu.VMEM((GY, *plane), F32),
            pltpu.VMEM((GY, *plane), F32),
            pltpu.VMEM((2, *plane), F32),
            pltpu.VMEM((GY, 2, *plane), F32),
            pltpu.VMEM((GY, 2, *plane), F32),
            pltpu.VMEM(groups, F32),
            pltpu.VMEM(groups, F32),
            pltpu.VMEM((2, 3, 8, 128), F32),
            pltpu.VMEM((3, 8, 128), F32),
            pltpu.VMEM(groups, F32),
            pltpu.VMEM((12, 8, 128), F32),
            dma((3,)), dma((8,)), dma((2,)), dma((2,)), dma((3,)), dma((3,)),
            dma((n,)), dma((n,)), dma((n,)), dma((n,)), dma((3,)), dma((3,)),
            dma((7,)), dma((7,)), dma((2,)), dma((2,)), dma((7,)), dma((7,)),
        ],
        compiler_params=pltpu.CompilerParams(
            collective_id=0, has_side_effects=True, vmem_limit_bytes=40 << 20
        ),
        name="exchange",
    )(*[pltpu.with_memory_space_constraint(x, pltpu.HBM) for x in (velocity_u, wall_strain, damping, high, low)])
    return pl.pallas_call(
        finish,
        out_shape=[jax.ShapeDtypeStruct(block, F32)] * 3,
        in_specs=[vmem] * 4,
        out_specs=[anywhere] * 3,
        scratch_shapes=[pltpu.VMEM(block, F32), pltpu.VMEM(block, F32), dma((6,))],
        compiler_params=pltpu.CompilerParams(vmem_limit_bytes=16 << 20),
        name="finish",
    )(*between)


def solution(mesh):
    spec = P("gx", None, "gy")
    return jax.shard_map(
        body,
        mesh=mesh,
        in_specs=(spec, spec, P(None, "gy")),
        out_specs=(spec, spec, spec),
        check_vma=False,
    )
```

time: 71.8 us -> 78.5 us (1.093)
  Pallas kernels: 71 us -> 77.8 us
    pallas_call x1, Pallas kernels: 68.3 us -> 75.1 us  [body(): pl.pallas_call(kernel, out_shape=[pltpu.VMEM(shape, F32) for shape in (bl...]
where the time goes in v3:
time: 78.5 us; the launch traced here: 78.4 us
  Pallas kernels  77.8 us (99%)
    pallas_call x1, Pallas kernels, body(): pl.pallas_call(kernel, out_shape=[pltpu.VMEM(shape, F32) for shape in (bl...  75.1 us
    pallas_call x1, Pallas kernels, body(): pl.pallas_call(finish, out_shape=[jax.ShapeDtypeStruct(block, F32)] * 3,...  2.7 us

profile of v3, /device:TPU:1, one launch (start us, length us, event | category | flops | bytes accessed | tf_op | source)
XLA Modules:
  0.0 78.4 jit_solution(14177019847861722680)
XLA Ops:
  0.6 75.1 %exchange.1 = (f32[64,16,512]{2,1,0:T(8,128)S(1)}, f32[64,16,512]{2,1,0:T(8,128)S(1)}, f32[2,16,512]{2,1,0:T(8,128)S(1)}, f32[8,2,8,128]{3,2,1,0:T(8,128)S(1)}) custom-call(f32[64,16,512]{2,1,0:T(8,128)} %u_hbm.1, f32[64,16,512]{2,1,0:T(8,128)} %w_hbm.1, f32[16,512]{1,0:T(8,128)} %damping_hbm.1, bf16[2048,2048]{1,0:T(8,128)(2,1)} %constant.4.clone.high_hbm, ...), custom_call_target="tpu_custom_call" | custom-call | tf_op jit(solution)/shard_map/exchange/pallas_call | solution.py:455
  75.7 2.7 %finish.1 = (f32[64,16,512]{2,1,0:T(8,128)}, f32[64,16,512]{2,1,0:T(8,128)}, f32[64,16,512]{2,1,0:T(8,128)}) custom-call(f32[64,16,512]{2,1,0:T(8,128)S(1)} %get-tuple-element.7.second, f32[64,16,512]{2,1,0:T(8,128)S(1)} %get-tuple-element.8.coeffs, f32[2,16,512]{2,1,0:T(8,128)S(1)} %get-tuple-element.9.factors, f32[8,2,8,128]{3,2,1,0:T(8,128)S(1)} %get-tuple-element.10.carried), custom_call_target="tpu_custom_call" | custom-call | tf_op jit(solution)/shard_map/finish/pallas_call | solution.py:491

commit v4 on v3

--- a/solution.py
+++ b/solution.py
@@ -59,7 +59,7 @@
     u_hbm, w_hbm, damping_hbm, high_hbm, low_hbm,
     second, coeffs, factors, carried,
     u, w, damping, source, rows, modes, table_hi, table_lo, lhs,
-    halo, all_damping, all_weight, sub, partial, arrived, lines, gathered, slabs, chain, back, small,
+    halo, all_damping, all_weight, sub, partial, arrived, lines, gathered, slabs, back, small,
     load_sem, table_sem, halo_send, halo_recv, damp_send, damp_recv, row_send, row_recv, mode_send, mode_recv,
     part_send, part_recv, a_send, a_recv, b_send, b_recv, c_send, c_recv,
 ):
@@ -72,7 +72,9 @@
     def in_slab(d):
         return {"gx": z * 8 + lax.rem(member + d, 8)}
 
-    above, below = {"gx": lax.rem(gx + 8, 64)}, {"gx": lax.rem(gx + 56, 64)}
+    def over_z(d):
+        return {"gx": lax.rem(z + d, 8) * 8 + member}
+
     following, previous = {"gx": lax.rem(gx + 1, 64)}, {"gx": lax.rem(gx + 63, 64)}
     out_up, out_down = jnp.logical_and(member == 7, z < 7), jnp.logical_and(member == 0, z > 0)
     barrier = pltpu.get_barrier_semaphore()
@@ -84,14 +86,15 @@
         greet(over_gy(d))
     for d in range(1, 8):
         greet(in_slab(d))
-    for needed, peer in ((z < 7, above), (z > 0, below), (out_up, following), (out_down, previous)):
+    for d in range(1, 8):
+        greet(over_z(d))
+    for needed, peer in ((out_up, following), (out_down, previous)):
 
         @pl.when(needed)
         def _(peer=peer):
             greet(peer)
 
-    greeted = 10 + (z < 7).astype(jnp.int32) + (z > 0).astype(jnp.int32)
-    greeted = greeted + out_up.astype(jnp.int32) + out_down.astype(jnp.int32)
+    greeted = 17 + out_up.astype(jnp.int32) + out_down.astype(jnp.int32)
 
     loads = [
         pltpu.make_async_copy(u_hbm, u, load_sem.at[0]),
@@ -326,58 +329,23 @@
     t_slab = tile
     for m in reversed(range(8)):
         t_slab = gathered[m, 1] + answer * seen[m] + scale * t_slab
-    slabs[1] = jnp.zeros((3, 8, 128), F32)
-
-    def up():
-        return pltpu.make_async_remote_copy(
-            src_ref=slabs.at[0, pl.ds(0, 1)], dst_ref=chain.at[pl.ds(0, 1)], send_sem=b_send.at[0],
-            recv_sem=b_recv.at[0], device_id=above, device_id_type=MESH,
-        )
-
-    def down():
-        return pltpu.make_async_remote_copy(
-            src_ref=slabs.at[0, pl.ds(1, 2)], dst_ref=chain.at[pl.ds(1, 2)], send_sem=b_send.at[1],
-            recv_sem=b_recv.at[1], device_id=below, device_id_type=MESH,
-        )
-
-    def pass_up():
-        @pl.when(z > 0)
-        def _():
-            up().wait_recv()
-            slabs[1, 0] = chain[0]
-
-        slabs[0, 0] = s_slab + slab_scale * slabs[1, 0]
-
-        @pl.when(z < 7)
-        def _():
-            up().start()
-
-    def pass_down():
-        @pl.when(z < 7)
-        def _():
-            down().wait_recv()
-            slabs[1, 1] = chain[1]
-            slabs[1, 2] = chain[2]
-
-        slabs[0, 1] = t_slab + slab_scale * (slabs[1, 1] + slabs[1, 2] * s_slab)
-        slabs[0, 2] = slab_answer + slab_scale * slab_scale * slabs[1, 2]
-
-        @pl.when(z > 0)
-        def _():
-            down().start()
-
-    @pl.when(z < 4)
-    def _():
-        pass_up()
-        pass_down()
-
-    @pl.when(z >= 4)
-    def _():
-        pass_down()
-        pass_up()
-
-    f = slabs[1, 0]
-    p = slabs[1, 1] + slabs[1, 2] * (s_slab + slab_scale * f)
+    slabs[z, 0] = s_slab
+    slabs[z, 1] = t_slab
+    b_copies = [
+        remote(slabs.at[z], slabs.at[z], b_send.at[d - 1], b_recv.at[d - 1], over_z(d)) for d in range(1, 8)
+    ]
+    for copy in b_copies:
+        copy.wait_recv()
+    f, seen = tile, []
+    for k in range(8):
+        seen.append(f)
+        small[12 + k] = f
+        f = slab_scale * f + slabs[k, 0]
+    p = tile
+    for k in reversed(range(8)):
+        small[20 + k] = p
+        p = slabs[k, 1] + slab_answer * seen[k] + slab_scale * p
+    f, p = small[12 + z], small[20 + z]
     seen = []
     for m in range(8):
         seen.append(f)
@@ -395,14 +363,6 @@
         copy.wait_recv()
     for copy in mode_copies.values():
         copy.wait_recv()
-
-    @pl.when(z < 7)
-    def _():
-        up().wait_send()
-
-    @pl.when(z > 0)
-    def _():
-        down().wait_send()
 
     for copy in started:
         copy.wait_send()
@@ -475,13 +435,12 @@
             pltpu.VMEM((GY, 2, *plane), F32),
             pltpu.VMEM(groups, F32),
             pltpu.VMEM(groups, F32),
-            pltpu.VMEM((2, 3, 8, 128), F32),
-            pltpu.VMEM((3, 8, 128), F32),
             pltpu.VMEM(groups, F32),
-            pltpu.VMEM((12, 8, 128), F32),
+            pltpu.VMEM(groups, F32),
+            pltpu.VMEM((28, 8, 128), F32),
             dma((3,)), dma((8,)), dma((2,)), dma((2,)), dma((3,)), dma((3,)),
             dma((n,)), dma((n,)), dma((n,)), dma((n,)), dma((3,)), dma((3,)),
-            dma((7,)), dma((7,)), dma((2,)), dma((2,)), dma((7,)), dma((7,)),
+            dma((7,)), dma((7,)), dma((7,)), dma((7,)), dma((7,)), dma((7,)),
         ],
         compiler_params=pltpu.CompilerParams(
             collective_id=0, has_side_effects=True, vmem_limit_bytes=40 << 20

time: 78.5 us -> 65.1 us (0.83)
  Pallas kernels: 77.8 us -> 63.8 us
    pallas_call x1, Pallas kernels: 75.1 us -> 61.1 us  [body(): pl.pallas_call(kernel, out_shape=[pltpu.VMEM(shape, F32) for shape in (bl...]
where the time goes in v4:
time: 65.1 us; the launch traced here: 64.4 us
  Pallas kernels  63.8 us (98%)
    pallas_call x1, Pallas kernels, body(): pl.pallas_call(kernel, out_shape=[pltpu.VMEM(shape, F32) for shape in (bl...  61.1 us
    pallas_call x1, Pallas kernels, body(): pl.pallas_call(finish, out_shape=[jax.ShapeDtypeStruct(block, F32)] * 3,...  2.7 us

profile of v4, /device:TPU:1, one launch (start us, length us, event | category | flops | bytes accessed | tf_op | source)
XLA Modules:
  0.0 64.4 jit_solution(17168548693147152847)
XLA Ops:
  0.6 61.1 %exchange.1 = (f32[64,16,512]{2,1,0:T(8,128)S(1)}, f32[64,16,512]{2,1,0:T(8,128)S(1)}, f32[2,16,512]{2,1,0:T(8,128)S(1)}, f32[8,2,8,128]{3,2,1,0:T(8,128)S(1)}) custom-call(f32[64,16,512]{2,1,0:T(8,128)} %u_hbm.1, f32[64,16,512]{2,1,0:T(8,128)} %w_hbm.1, f32[16,512]{1,0:T(8,128)} %damping_hbm.1, bf16[2048,2048]{1,0:T(8,128)(2,1)} %constant.4.clone.high_hbm, ...), custom_call_target="tpu_custom_call" | custom-call | tf_op jit(solution)/shard_map/exchange/pallas_call | solution.py:415
  61.7 2.7 %finish.1 = (f32[64,16,512]{2,1,0:T(8,128)}, f32[64,16,512]{2,1,0:T(8,128)}, f32[64,16,512]{2,1,0:T(8,128)}) custom-call(f32[64,16,512]{2,1,0:T(8,128)S(1)} %get-tuple-element.7.second, f32[64,16,512]{2,1,0:T(8,128)S(1)} %get-tuple-element.8.coeffs, f32[2,16,512]{2,1,0:T(8,128)S(1)} %get-tuple-element.9.factors, f32[8,2,8,128]{3,2,1,0:T(8,128)S(1)} %get-tuple-element.10.carried), custom_call_target="tpu_custom_call" | custom-call | tf_op jit(solution)/shard_map/finish/pallas_call | solution.py:450

commit v5 on v4

--- a/solution.py
+++ b/solution.py
@@ -59,8 +59,8 @@
     u_hbm, w_hbm, damping_hbm, high_hbm, low_hbm,
     second, coeffs, factors, carried,
     u, w, damping, source, rows, modes, table_hi, table_lo, lhs,
-    halo, all_damping, all_weight, sub, partial, arrived, lines, gathered, slabs, back, small,
-    load_sem, table_sem, halo_send, halo_recv, damp_send, damp_recv, row_send, row_recv, mode_send, mode_recv,
+    halo, damp_tiles, all_damping, all_weight, sub, partial, arrived, lines, gathered, slabs, back, small,
+    load_sem, table_sem, halo_send, halo_recv, damp_send, damp_recv, share_send, share_recv, row_send, row_recv, mode_send, mode_recv,
     part_send, part_recv, a_send, a_recv, b_send, b_recv, c_send, c_recv,
 ):
     gx, gy = lax.axis_index("gx"), lax.axis_index("gy")
@@ -188,6 +188,12 @@
     for copy in tables:
         copy.start()
     inner_chunk(r0)
+    lam = damping[...]
+    factors[0] = lam
+    factors[1] = weight_of(lam)
+    for g in range(8):
+        small[g] = lam[8 * (g // 4) : 8 * (g // 4) + 8, 128 * (g % 4) : 128 * (g % 4) + 128]
+    damp_tiles[member, gy] = small[member]
     pl.semaphore_wait(barrier, greeted)
 
     def halo_copy(k):
@@ -208,13 +214,11 @@
     def _():
         halo_copy(1).start()
 
+    own_tile = damp_tiles.at[member, gy]
+    damps = [remote(own_tile, own_tile, damp_send.at[d - 1], damp_recv.at[d - 1], over_gy(d)) for d in range(1, GY)]
     send_rows(r0)
     inner_chunk(r1)
     send_rows(r1)
-    damps = [
-        remote(damping, all_damping.at[gy], damp_send.at[d - 1], damp_recv.at[d - 1], over_gy(d)) for d in range(1, GY)
-    ]
-    all_damping[gy] = damping[...]
     inner_chunk(r2)
     inner_chunk(r3)
 
@@ -253,19 +257,21 @@
     for i in (CELLS - 3, CELLS - 2, CELLS - 1):
         edge(i)
     send_rows(r3)
-
-    lam = damping[...]
-    factors[0] = lam
-    factors[1] = weight_of(lam)
-    for g in range(8):
-        small[g] = lam[8 * (g // 4) : 8 * (g // 4) + 8, 128 * (g % 4) : 128 * (g % 4) + 128]
+    for copy in damps:
+        copy.wait_recv()
+    own_group = damp_tiles.at[member]
+    shares = [remote(own_group, own_group, share_send.at[d - 1], share_recv.at[d - 1], in_slab(d)) for d in range(1, 8)]
+
     for k, value in enumerate(response(lam, 4)):
         sub[k] = value
     for k, value in enumerate((*response(small[member], 6), *response(small[member], 9))):
         small[8 + k] = value
-    for copy in damps:
+    for copy in shares:
         copy.wait_recv()
     for o in range(GY):
+        for g in range(8):
+            at = slice(8 * (g // 4), 8 * (g // 4) + 8), slice(128 * (g % 4), 128 * (g % 4) + 128)
+            all_damping[(o, *at)] = damp_tiles[g, o]
         all_weight[o] = weight_of(all_damping[o])
     for copy in tables:
         copy.wait()
@@ -428,6 +434,7 @@
             pltpu.VMEM((NY, NY), BF16),
             pltpu.VMEM((2 * STEP * PLANES, NY), BF16),
             pltpu.VMEM((2, 3, *plane), F32),
+            pltpu.VMEM((8, GY, 8, 128), F32),
             pltpu.VMEM((GY, *plane), F32),
             pltpu.VMEM((GY, *plane), F32),
             pltpu.VMEM((2, *plane), F32),
@@ -438,7 +445,7 @@
             pltpu.VMEM(groups, F32),
             pltpu.VMEM(groups, F32),
             pltpu.VMEM((28, 8, 128), F32),
-            dma((3,)), dma((8,)), dma((2,)), dma((2,)), dma((3,)), dma((3,)),
+            dma((3,)), dma((8,)), dma((2,)), dma((2,)), dma((3,)), dma((3,)), dma((7,)), dma((7,)),
             dma((n,)), dma((n,)), dma((n,)), dma((n,)), dma((3,)), dma((3,)),
             dma((7,)), dma((7,)), dma((7,)), dma((7,)), dma((7,)), dma((7,)),
         ],

time: 65.1 us -> 64 us (0.983)
  Pallas kernels: 63.8 us -> 62.7 us
    pallas_call x1, Pallas kernels: 61.1 us -> 60 us  [body(): pl.pallas_call(kernel, out_shape=[pltpu.VMEM(shape, F32) for shape in (bl...]
where the time goes in v5:
time: 64 us; the launch traced here: 63.4 us
  Pallas kernels  62.7 us (98%)
  between operations  0.64 us (1%)
    pallas_call x1, Pallas kernels, body(): pl.pallas_call(kernel, out_shape=[pltpu.VMEM(shape, F32) for shape in (bl...  60 us
    pallas_call x1, Pallas kernels, body(): pl.pallas_call(finish, out_shape=[jax.ShapeDtypeStruct(block, F32)] * 3,...  2.7 us

profile of v5, /device:TPU:1, one launch (start us, length us, event | category | flops | bytes accessed | tf_op | source)
XLA Modules:
  0.0 63.4 jit_solution(13575715665696208856)
XLA Ops:
  0.6 60.0 %exchange.1 = (f32[64,16,512]{2,1,0:T(8,128)S(1)}, f32[64,16,512]{2,1,0:T(8,128)S(1)}, f32[2,16,512]{2,1,0:T(8,128)S(1)}, f32[8,2,8,128]{3,2,1,0:T(8,128)S(1)}) custom-call(f32[64,16,512]{2,1,0:T(8,128)} %u_hbm.1, f32[64,16,512]{2,1,0:T(8,128)} %w_hbm.1, f32[16,512]{1,0:T(8,128)} %damping_hbm.1, bf16[2048,2048]{1,0:T(8,128)(2,1)} %constant.4.clone.high_hbm, ...), custom_call_target="tpu_custom_call" | custom-call | tf_op jit(solution)/shard_map/exchange/pallas_call | solution.py:421
  60.6 2.7 %finish.1 = (f32[64,16,512]{2,1,0:T(8,128)}, f32[64,16,512]{2,1,0:T(8,128)}, f32[64,16,512]{2,1,0:T(8,128)}) custom-call(f32[64,16,512]{2,1,0:T(8,128)S(1)} %get-tuple-element.7.second, f32[64,16,512]{2,1,0:T(8,128)S(1)} %get-tuple-element.8.coeffs, f32[2,16,512]{2,1,0:T(8,128)S(1)} %get-tuple-element.9.factors, f32[8,2,8,128]{3,2,1,0:T(8,128)S(1)} %get-tuple-element.10.carried), custom_call_target="tpu_custom_call" | custom-call | tf_op jit(solution)/shard_map/finish/pallas_call | solution.py:457

commit v6 on v5

--- a/solution.py
+++ b/solution.py
@@ -98,9 +98,14 @@
 
     loads = [
         pltpu.make_async_copy(u_hbm, u, load_sem.at[0]),
-        pltpu.make_async_copy(w_hbm, w, load_sem.at[1]),
-        pltpu.make_async_copy(damping_hbm, damping, load_sem.at[2]),
+        pltpu.make_async_copy(damping_hbm, damping, load_sem.at[1]),
     ]
+    strain = {}
+    for q in ROUNDS:
+        for j in range(GY):
+            here = pl.ds(j * OWN + q * STEP, STEP)
+            strain[q, j] = pltpu.make_async_copy(w_hbm.at[here], w.at[here], load_sem.at[2 + q * GY + j])
+    loads += [strain[ROUNDS[0], j] for j in range(GY)]
     tables = []
     for d in range(GY):
         block = pl.ds(pl.multiple_of(lax.rem(gy + GY - d, GY) * COLS, COLS), COLS)
@@ -182,10 +187,10 @@
         coeffs[pl.ds(gy * OWN + q * STEP, STEP)] = modes[gy, q * STEP : (q + 1) * STEP]
 
     r0, r1, r2, r3 = ROUNDS
-    loads[0].wait()
-    loads[1].wait()
-    loads[2].wait()
-    for copy in tables:
+    for copy in loads:
+        copy.wait()
+    others = [strain[q, j] for q in ROUNDS[1:] for j in range(GY)]
+    for copy in others + tables:
         copy.start()
     inner_chunk(r0)
     lam = damping[...]
@@ -217,6 +222,8 @@
     own_tile = damp_tiles.at[member, gy]
     damps = [remote(own_tile, own_tile, damp_send.at[d - 1], damp_recv.at[d - 1], over_gy(d)) for d in range(1, GY)]
     send_rows(r0)
+    for copy in others:
+        copy.wait()
     inner_chunk(r1)
     send_rows(r1)
     inner_chunk(r2)
@@ -283,7 +290,9 @@
     transform(r3)
 
     blank = jnp.zeros((PLANES, COLS), F32)
-    for o in range(GY):
+    parts = []
+    for d in (1, 2, 3, 0):
+        o = lax.rem(gy + d, GY)
 
         def own_rows(i, carry, o=o):
             s, t, power = carry
@@ -291,16 +300,13 @@
             return s, t + power * s, power * all_damping[o]
 
         s, t, _ = lax.fori_loop(0, OWN, own_rows, (blank, blank, blank + 1.0), unroll=2)
-        partial[o, 0] = s
-        partial[o, 1] = t
-    parts = [
-        remote(
-            partial.at[lax.rem(gy + d, GY)], arrived.at[gy], part_send.at[d - 1], part_recv.at[d - 1],
-            over_gy(d),
-        )
-        for d in range(1, GY)
-    ]
-    arrived[gy] = partial[gy]
+        if d:
+            partial[o, 0] = s
+            partial[o, 1] = t
+            parts.append(remote(partial.at[o], arrived.at[gy], part_send.at[d - 1], part_recv.at[d - 1], over_gy(d)))
+        else:
+            arrived[gy, 0] = s
+            arrived[gy, 1] = t
     send_modes(r1)
     send_modes(r2)
 
@@ -445,7 +451,7 @@
             pltpu.VMEM(groups, F32),
             pltpu.VMEM(groups, F32),
             pltpu.VMEM((28, 8, 128), F32),
-            dma((3,)), dma((8,)), dma((2,)), dma((2,)), dma((3,)), dma((3,)), dma((7,)), dma((7,)),
+            dma((18,)), dma((8,)), dma((2,)), dma((2,)), dma((3,)), dma((3,)), dma((7,)), dma((7,)),
             dma((n,)), dma((n,)), dma((n,)), dma((n,)), dma((3,)), dma((3,)),
             dma((7,)), dma((7,)), dma((7,)), dma((7,)), dma((7,)), dma((7,)),
         ],

time: 64 us -> 64.2 us (level)
  no operation moved by 1% of the time
where the time goes in v6:
time: 64.2 us; the launch traced here: 63.4 us
  Pallas kernels  62.7 us (98%)
    pallas_call x1, Pallas kernels, body(): pl.pallas_call(kernel, out_shape=[pltpu.VMEM(shape, F32) for shape in (bl...  60 us
    pallas_call x1, Pallas kernels, body(): pl.pallas_call(finish, out_shape=[jax.ShapeDtypeStruct(block, F32)] * 3,...  2.7 us

profile of v6, /device:TPU:1, one launch (start us, length us, event | category | flops | bytes accessed | tf_op | source)
XLA Modules:
  0.0 63.4 jit_solution(12983596130404807934)
XLA Ops:
  0.6 60.0 %exchange.1 = (f32[64,16,512]{2,1,0:T(8,128)S(1)}, f32[64,16,512]{2,1,0:T(8,128)S(1)}, f32[2,16,512]{2,1,0:T(8,128)S(1)}, f32[8,2,8,128]{3,2,1,0:T(8,128)S(1)}) custom-call(f32[64,16,512]{2,1,0:T(8,128)} %u_hbm.1, f32[64,16,512]{2,1,0:T(8,128)} %w_hbm.1, f32[16,512]{1,0:T(8,128)} %damping_hbm.1, bf16[2048,2048]{1,0:T(8,128)(2,1)} %constant.4.clone.high_hbm, ...), custom_call_target="tpu_custom_call" | custom-call | tf_op jit(solution)/shard_map/exchange/pallas_call | solution.py:427
  60.7 2.7 %finish.1 = (f32[64,16,512]{2,1,0:T(8,128)}, f32[64,16,512]{2,1,0:T(8,128)}, f32[64,16,512]{2,1,0:T(8,128)}) custom-call(f32[64,16,512]{2,1,0:T(8,128)S(1)} %get-tuple-element.7.second, f32[64,16,512]{2,1,0:T(8,128)S(1)} %get-tuple-element.8.coeffs, f32[2,16,512]{2,1,0:T(8,128)S(1)} %get-tuple-element.9.factors, f32[8,2,8,128]{3,2,1,0:T(8,128)S(1)} %get-tuple-element.10.carried), custom_call_target="tpu_custom_call" | custom-call | tf_op jit(solution)/shard_map/finish/pallas_call | solution.py:463
